TPU v7x, 32 devices: a whole 2x2x4 slice. The times are simulated.
32 devices in a mesh: feat: 8 (over z, core), node: 4 (over y, x).
Axes of the slice: x: 2, y: 2, z: 4, core: 2. Of those that a mesh axis runs over, the one named last changes fastest.
Arguments:
- node_features: bfloat16 [1024, 4, 1024], P('feat', 'node'), may hold values from -6 to 6
- weight: bfloat16 [1024, 256], P('feat'), may hold values from -0.1875 to 0.1875
- out_bias: float32 [256], replicated, may hold values from -3 to 3
- edge_tiles: bfloat16 [4, 8, 8, 128, 128], P('node', 'feat'), may hold values from 0.049804688 to 1
- tile_column: int32 [4, 8, 8], P('node', 'feat'), may hold values from 0 to 7, as said below
- tile_count: int32 [4, 8], P('node', 'feat'), may hold values from 1 to 8, as said below
- grad_hidden: bfloat16 [4, 1024, 256], P('node', 'feat'), may hold values from -6 to 6
Outputs:
- hidden: bfloat16 [4, 1024, 256], P('node', 'feat')
- grad_features: bfloat16 [1024, 4, 1024], P('feat', 'node')
- weight_grad: float32 [1024, 256], P('feat')
Inputs may be any that keep to these rules, and one draw needn't show every extreme that they name: `tile_column`: the 8 column blocks listed for one row block are distinct, live slots or not. `tile_count`: slots of a row block beyond its count are ignored. In every cluster some row block has exactly 8 live tiles.
All inputs are finite; a program needn't handle non-finite values.
Results may differ from a plain program's by a relative error of at most 0.007.
Values may be sent and summed in bfloat16 or wider, within the bound.
A program may use at most 64 MiB of HBM per device.

v0:
```python
import math
import jax
import jax.numpy as jnp
from jax import lax
from jax.sharding import PartitionSpec as P


def gelu_tanh(pre_value):
    return jax.nn.gelu(pre_value, approximate=True)


def body(node_features, weight, out_bias, edge_tiles, tile_column, tile_count, grad_hidden):
    feat_dev, clusters, cluster_rows = node_features.shape
    blocks = lax.axis_size("feat")
    tile_rows = cluster_rows // blocks
    hidden_width = weight.shape[1]
    summed_rows = lax.psum_scatter(
        jnp.einsum("fqr,fh->rqh", node_features, weight, preferred_element_type=jnp.float32),
        "feat",
        scatter_dimension=0,
        tiled=True,
    )
    own_proj = jnp.transpose(summed_rows, (1, 0, 2))
    own_rounded = own_proj.astype(jnp.bfloat16)
    all_proj = lax.all_gather(own_rounded, "feat", axis=1, tiled=True)
    blocks_proj = all_proj.reshape(clusters, blocks, tile_rows, hidden_width)
    my_tiles = edge_tiles[:, 0]
    my_cols = tile_column[:, 0]
    counts = tile_count[:, 0]
    slot_ids = jnp.arange(my_tiles.shape[1], dtype=jnp.int32)
    live_mask = (slot_ids[None, :] < counts[:, None]).astype(jnp.bfloat16)
    masked = my_tiles * live_mask[:, :, None, None]
    degree = jnp.sum(masked, axis=(1, 3), dtype=jnp.float32)
    cluster_ids = jnp.arange(clusters, dtype=jnp.int32)[:, None]
    chosen = blocks_proj[cluster_ids, my_cols]
    summed = jnp.einsum("qsij,qsjh->qih", masked, chosen, preferred_element_type=jnp.float32)
    row_scale = lax.rsqrt(degree)[:, :, None]
    pre_act = summed * row_scale + out_bias
    activated, backward = jax.vjp(gelu_tanh, pre_act)
    hidden = activated.astype(jnp.bfloat16)
    (grad_pre,) = backward(grad_hidden.astype(jnp.float32))
    scaled = (grad_pre * row_scale).astype(jnp.bfloat16)
    tile_terms = jnp.einsum(
        "qsij,qih->qsjh", masked, scaled, preferred_element_type=jnp.float32
    ).astype(jnp.bfloat16)
    outgoing = (
        jnp.zeros((blocks, clusters, tile_rows, hidden_width), jnp.bfloat16)
        .at[my_cols, cluster_ids]
        .set(tile_terms)
    )
    arrived = lax.all_to_all(outgoing, "feat", split_axis=0, concat_axis=0, tiled=True)
    own_grad = jnp.sum(arrived, axis=0, dtype=jnp.float32).astype(jnp.bfloat16)
    all_grad = lax.all_gather(own_grad, "feat", axis=1, tiled=True)
    grad_features = jnp.einsum(
        "fh,qrh->fqr", weight, all_grad, preferred_element_type=jnp.float32
    ).astype(jnp.bfloat16)
    partial_grad = jnp.einsum(
        "fqr,qrh->fh", node_features, all_grad, preferred_element_type=jnp.float32
    )
    total_nodes = clusters * lax.axis_size("node") * cluster_rows
    weight_grad = lax.psum(partial_grad, "node") * (1.0 / math.sqrt(total_nodes))
    return (hidden, grad_features, weight_grad)


def solution(mesh):
    return jax.shard_map(
        body,
        mesh=mesh,
        in_specs=(
            P("feat", "node", None),
            P("feat", None),
            P(),
            P("node", "feat", None, None, None),
            P("node", "feat", None),
            P("node", "feat"),
            P("node", "feat", None),
        ),
        out_specs=(P("node", "feat", None), P("feat", "node", None), P("feat", None)),
        check_vma=False,
    )
```

profile of v0, /device:TPU:0, one launch (start us, length us, event | category | flops | bytes accessed | tf_op | source)
XLA Modules:
  0.0 150.2 jit_solution(10850708865901555610)
XLA Ops:
  7.2 0.0 copy-start
  7.2 0.0 reduce-scatter.2.cloned.1.call-start
  7.2 0.9 copy-done
  8.1 2.1 %convolution_bitcast_fusion = f32[1024,1,256]{0,2,1:T(8,128)} fusion(bf16[128,256]{1,0:T(8,128)(2,1)} %param.8, bf16[128,1,1024]{2,0,1:T(8,128)(2,1)S(1)} %copy-done), kind=kOutput, calls=%fused_computation.2 | convolution fusion | flops 67108864 | bytes 1376256 | tf_op jit(solution)/shard_map/fqr,fh->rqh/dot_general | solution.py:18
  10.3 0.0 copy-start.1
  10.3 0.0 reduce-scatter.2.cloned.1.call-update
  11.0 0.2 copy-done.1
  11.2 0.2 convert_reduce_fusion
  11.4 0.0 copy-start.5
  11.4 0.6 copy-done.5
  12.1 33.3 %reduce-scatter.2.cloned.1.call-done = f32[128,1,256]{0,2,1:T(8,128)} async-done(((f32[1024,1,256]{0,2,1:T(8,128)}), f32[128,1,256]{0,2,1:T(8,128)}) %reduce-scatter.2.cloned.1.call-update) | async-done | bytes 131088 | tf_op jit(solution)/shard_map/reduce_scatter | solution.py:17
  45.5 0.9 convert_element_type.64
  46.4 14.0 %all-gather = bf16[1024,1,256]{0,2,1:T(8,128)(2,1)S(1)} all-gather(bf16[128,1,256]{0,2,1:T(8,128)(2,1)S(1)} %convert_element_type.64), channel_id=2, replica_groups=mesh['feat'=8,'node'=4] {'feat'}, dimensions={0}, use_global_device_ids=true | all-gather | bytes 589824 | tf_op jit(solution)/shard_map/all_gather | solution.py:25
  60.4 0.2 copy.22
  60.6 0.0 copy-start.3
  60.6 0.6 gather_fusion
  61.2 0.1 copy-done.3
  61.3 0.0 copy-start.4
  61.3 0.3 fusion.2
  61.5 0.6 copy-done.4
  62.1 0.4 convolution_convert_fusion
  62.5 0.8 broadcast.100
  63.4 2.5 %scatter_fusion = bf16[8,128,256]{2,1,0:T(8,128)(2,1)} fusion(bf16[8,128,256]{2,1,0:T(8,128)(2,1)} %broadcast.100, s32[8]{0:T(128)S(1)} %fusion.32, bf16[8,128,256]{2,1,0:T(8,128)(2,1)S(1)} %convolution_convert_fusion), kind=kCustom, calls=%fused_computation.1 | custom fusion | bytes 1572896 | tf_op jit(solution)/shard_map/scatter | solution.py:49
  65.8 3.5 %all-to-all-start = ((bf16[8,1,128,256]{3,2,1,0:T(8,128)(2,1)}), bf16[8,1,128,256]{3,2,1,0:T(8,128)(2,1)S(1)}, u32[]{:S(2)}, u32[]{:S(2)}) async-start(bf16[8,1,128,256]{3,2,1,0:T(8,128)(2,1)} %bitcast.21), calls=%async_computation.1 | async-start | bytes 1048576 | tf_op jit(solution)/shard_map/all_to_all | solution.py:51
  69.3 0.0 all-reduce.4.cloned.1.call-start
  69.4 0.7 fusion.31
  70.0 14.6 %all-to-all-done = bf16[8,1,128,256]{3,2,1,0:T(8,128)(2,1)S(1)} async-done(((bf16[8,1,128,256]{3,2,1,0:T(8,128)(2,1)}), bf16[8,1,128,256]{3,2,1,0:T(8,128)(2,1)S(1)}, u32[]{:S(2)}, u32[]{:S(2)}) %all-to-all-start) | async-done | bytes 524320 | tf_op jit(solution)/shard_map/all_to_all | solution.py:51
  84.6 0.1 reduce_sum.24
  84.7 14.9 %all-gather.1 = bf16[1024,256]{1,0:T(8,128)(2,1)S(1)} all-gather(bf16[128,256]{1,0:T(8,128)(2,1)S(1)} %reduce_sum.24), channel_id=3, replica_groups=mesh['feat'=8,'node'=4] {'feat'}, dimensions={0}, use_global_device_ids=true | all-gather | bytes 589824 | tf_op jit(solution)/shard_map/all_gather | solution.py:53
  99.6 1.0 convolution_bitcast_fusion.1
  100.6 0.0 copy-start.2
  100.6 0.0 all-reduce.4.cloned.1.call-update
  100.6 0.8 copy-done.2
  101.5 0.3 fusion
  101.8 0.9 copy.19
  102.6 39.1 %all-reduce.4.cloned.1.call-done = f32[128,256]{0,1:T(8,128)} async-done(((f32[128,256]{0,1:T(8,128)}), f32[128,256]{0,1:T(8,128)}) %all-reduce.4.cloned.1.call-update) | async-done | bytes 131088 | tf_op jit(solution)/shard_map/psum | solution.py:61
  141.7 0.9 broadcast_multiply_fusion
  142.6 0.8 copy.20
  (6 shorter events, 0.0 us)
Async XLA Ops:
  7.2 1.0 copy-start
  7.2 38.3 %reduce-scatter.2.cloned.1.call-start = ((), (), s32[]{:S(2)}) async-start(), calls=%async_computation.2 | async-start | bytes 1179648 | tf_op jit(solution)/shard_map/reduce_scatter | solution.py:17
  10.3 1.0 copy-start.1
  11.4 0.7 copy-start.5
  60.6 0.7 copy-start.3
  61.3 0.8 copy-start.4
  65.8 18.8 %all-to-all-start = ((bf16[8,1,128,256]{3,2,1,0:T(8,128)(2,1)}), bf16[8,1,128,256]{3,2,1,0:T(8,128)(2,1)S(1)}, u32[]{:S(2)}, u32[]{:S(2)}) async-start(bf16[8,1,128,256]{3,2,1,0:T(8,128)(2,1)} %bitcast.21), calls=%async_computation.1 | async-start | bytes 1048576 | tf_op jit(solution)/shard_map/all_to_all | solution.py:51
  69.3 72.4 %all-reduce.4.cloned.1.call-start = ((), (), s32[]{:S(2)}) async-start(), calls=%async_computation.3 | async-start | bytes 262144 | tf_op jit(solution)/shard_map/psum | solution.py:61
  100.6 0.8 copy-start.2
Sparse Core Ops, SparseCore 0:
  10.4 35.0 reduce-scatter.1
  100.8 40.8 all-reduce.3
where the time goes:
time: 151 us; the launch traced here: 150 us
  waiting for transfers between devices  87 us (58%)
  blocking collectives  28.9 us (19%)
  between operations  14.8 us (10%)
  local copies, waits for them, and re-layouts  8.93 us (6%)
  matrix products  4.12 us (3%)
  starting transfers between devices  3.57 us (2%)
  other arithmetic  2.8 us (2%)
    psum x1, waiting for transfers between devices, body(): lax.psum(partial_grad, 'node') * (1.0 / math.sqrt(total_nodes))  39.1 us
    reduce_scatter x1, waiting for transfers between devices, body(): lax.psum_scatter(jnp.einsum('fqr,fh->rqh', node_features, weight, preferr...  33.3 us
    all_gather x1, blocking collectives, body(): all_grad = lax.all_gather(own_grad, 'feat', axis=1, tiled=True)  14.9 us
    all_to_all x1, waiting for transfers between devices, body(): lax.all_to_all(outgoing, 'feat', split_axis=0, concat_axis=0, tiled=True)  14.6 us
    all_gather x1, blocking collectives, body(): all_proj = lax.all_gather(own_rounded, 'feat', axis=1, tiled=True)  14 us
    unnamed x14, local copies, waits for them, and re-layouts  4.86 us
    all_to_all x1, starting transfers between devices, body(): lax.all_to_all(outgoing, 'feat', split_axis=0, concat_axis=0, tiled=True)  3.49 us
  transfers between devices with their start and end apart: 3, of which 3 were waited for; matrix products, arithmetic and copies ran while one was open for 1% of the time, Pallas kernels for 0%

commit v1 on v0

--- a/solution.py
+++ b/solution.py
@@ -3,6 +3,12 @@
 import jax.numpy as jnp
 from jax import lax
 from jax.sharding import PartitionSpec as P
+
+
+def process_the_runs(unit, row_dim):
+    later = list(unit.shape[1:])
+    later[row_dim] *= unit.shape[0]
+    return jnp.moveaxis(unit, 0, row_dim).reshape(later)
 
 
 def gelu_tanh(pre_value):
@@ -50,7 +56,23 @@
     )
     arrived = lax.all_to_all(outgoing, "feat", split_axis=0, concat_axis=0, tiled=True)
     own_grad = jnp.sum(arrived, axis=0, dtype=jnp.float32).astype(jnp.bfloat16)
-    all_grad = lax.all_gather(own_grad, "feat", axis=1, tiled=True)
+    n_dev_all = lax.axis_size("feat")
+    blocks_here = [(k0, (k0 + 1) % n_dev_all) for k0 in range(n_dev_all)]
+    trail = [(src_i, no) for no, src_i in blocks_here]
+    g_now, v_next = ([], [])
+    for w in tuple(range(n_dev_all - 1)):
+        if w % 2 == 0:
+            g_now.append(
+                lax.ppermute(g_now[-1] if g_now else own_grad, perm=blocks_here, axis_name="feat")
+            )
+        else:
+            v_next.append(
+                lax.ppermute(v_next[-1] if v_next else own_grad, axis_name="feat", perm=trail)
+            )
+    y = jnp.stack([*g_now[::-1], own_grad, *v_next])
+    x_now = lax.axis_index("feat") - len(g_now)
+    y = y[(jnp.arange(n_dev_all) - x_now) % n_dev_all]
+    all_grad = process_the_runs(y, 1)
     grad_features = jnp.einsum(
         "fh,qrh->fqr", weight, all_grad, preferred_element_type=jnp.float32
     ).astype(jnp.bfloat16)

time: 151 us -> 158 us (1.046)
  starting transfers between devices: 3.57 us -> 10.9 us
  blocking collectives: 28.9 us -> 31.8 us
  local copies, waits for them, and re-layouts: 8.93 us -> 7.05 us
    all_to_all x0 -> x1, blocking collectives: none -> 17.8 us  [body(): lax.all_to_all(outgoing, 'feat', split_axis=0, concat_axis=0, tiled=True)]
    all_gather x1 -> x0, blocking collectives: 14.9 us -> none  [body(): all_grad = lax.all_gather(own_grad, 'feat', axis=1, tiled=True)]
    all_to_all x1 -> x0, waiting for transfers between devices: 14.6 us -> none  [body(): lax.all_to_all(outgoing, 'feat', split_axis=0, concat_axis=0, tiled=True)]
    ppermute x0 -> x7, waiting for transfers between devices: none -> 11.2 us  [the longest x4 10.6 us: body(): lax.ppermute(g_now[-1] if g_now else own_grad, perm=blocks_here, axis_nam...]
    ppermute x0 -> x7, starting transfers between devices: none -> 10.8 us  [the longest x3 10.7 us: body(): lax.ppermute(v_next[-1] if v_next else own_grad, axis_name='feat', perm=t...]
    all_to_all x1 -> x0, starting transfers between devices: 3.49 us -> none  [body(): lax.all_to_all(outgoing, 'feat', split_axis=0, concat_axis=0, tiled=True)]
    psum x1, waiting for transfers between devices: 39.1 us -> 41.5 us  [body(): lax.psum(partial_grad, 'node') * (1.0 / math.sqrt(total_nodes))]
    scatter x1, local copies, waits for them, and re-layouts: 2.46 us -> 0.78 us  [body(): outgoing = jnp.zeros((blocks, clusters, tile_rows, hidden_width), jnp.bfl...]
  transfers between devices with their start and end apart: 3 -> 9, of which waited for: 3 -> 7; matrix products, arithmetic and copies ran while one was open for 1% -> 1% of each run, Pallas kernels for 0% -> 0%
where the time goes in v1:
time: 158 us
  waiting for transfers between devices  86.1 us (54%)
  blocking collectives  31.8 us (20%)
  between operations  14.9 us (9%)
  starting transfers between devices  10.9 us (7%)
  local copies, waits for them, and re-layouts  7.05 us (4%)
  matrix products  4.12 us (3%)
  other arithmetic  2.82 us (2%)
    psum x1, waiting for transfers between devices, body(): lax.psum(partial_grad, 'node') * (1.0 / math.sqrt(total_nodes))  41.5 us
    reduce_scatter x1, waiting for transfers between devices, body(): lax.psum_scatter(jnp.einsum('fqr,fh->rqh', node_features, weight, preferr...  33.4 us
    all_to_all x1, blocking collectives, body(): lax.all_to_all(outgoing, 'feat', split_axis=0, concat_axis=0, tiled=True)  17.8 us
    all_gather x1, blocking collectives, body(): all_proj = lax.all_gather(own_rounded, 'feat', axis=1, tiled=True)  14 us
    ppermute x3, starting transfers between devices, body(): lax.ppermute(v_next[-1] if v_next else own_grad, axis_name='feat', perm=t...  10.7 us
    ppermute x4, waiting for transfers between devices, body(): lax.ppermute(g_now[-1] if g_now else own_grad, perm=blocks_here, axis_nam...  10.6 us
    unnamed x21, local copies, waits for them, and re-layouts  4.84 us
  transfers between devices with their start and end apart: 9, of which 7 were waited for; matrix products, arithmetic and copies ran while one was open for 1% of the time, Pallas kernels for 0%

profile of v1, /device:TPU:0, one launch (start us, length us, event | category | flops | bytes accessed | tf_op | source)
XLA Modules:
  0.0 157.6 jit_solution(7951356761808314328)
XLA Ops:
  7.2 0.0 copy-start
  7.2 0.0 reduce-scatter.2.cloned.1.call-start
  7.2 0.9 copy-done
  8.1 2.1 %convolution_bitcast_fusion = f32[1024,1,256]{0,2,1:T(8,128)} fusion(bf16[128,256]{1,0:T(8,128)(2,1)} %param.8, bf16[128,1,1024]{2,0,1:T(8,128)(2,1)S(1)} %copy-done), kind=kOutput, calls=%fused_computation.3 | convolution fusion | flops 67108864 | bytes 1376256 | tf_op jit(solution)/shard_map/fqr,fh->rqh/dot_general | solution.py:24
  10.2 0.0 copy-start.1
  10.2 0.0 reduce-scatter.2.cloned.1.call-update
  10.3 0.0 all-reduce.4.cloned.1.call-start
  11.0 0.2 copy-done.1
  11.2 0.2 convert_reduce_fusion
  11.4 0.0 copy-start.5
  11.4 0.6 copy-done.5
  12.1 33.4 %reduce-scatter.2.cloned.1.call-done = f32[128,1,256]{0,2,1:T(8,128)} async-done(((f32[1024,1,256]{0,2,1:T(8,128)}), f32[128,1,256]{0,2,1:T(8,128)}) %reduce-scatter.2.cloned.1.call-update) | async-done | bytes 131088 | tf_op jit(solution)/shard_map/reduce_scatter | solution.py:23
  45.5 0.9 convert_element_type.64
  46.4 14.0 %all-gather = bf16[1024,1,256]{0,2,1:T(8,128)(2,1)S(1)} all-gather(bf16[128,1,256]{0,2,1:T(8,128)(2,1)S(1)} %convert_element_type.64), channel_id=2, replica_groups=mesh['feat'=8,'node'=4] {'feat'}, dimensions={0}, use_global_device_ids=true | all-gather | bytes 589824 | tf_op jit(solution)/shard_map/all_gather | solution.py:31
  60.4 0.2 copy.22
  60.6 0.0 copy-start.3
  60.6 0.6 gather_fusion
  61.2 0.1 copy-done.3
  61.3 0.3 fusion.2
  61.5 0.6 copy-done.4
  62.1 0.4 convolution_convert_fusion
  62.6 0.8 scatter_fusion
  63.4 17.8 %all_to_all.5 = bf16[8,1,128,256]{3,2,1,0:T(8,128)(2,1)S(1)} all-to-all(bf16[8,1,128,256]{3,2,1,0:T(8,128)(2,1)S(1)} %bitcast.105), channel_id=1, replica_groups=mesh['feat'=8,'node'=4] {'feat'}, dimensions={0} | all-to-all | bytes 1048576 | tf_op jit(solution)/shard_map/all_to_all | solution.py:57
  81.1 0.1 reduce_sum.24
  81.2 0.1 collective-permute-start
  81.3 5.5 %collective-permute-done = bf16[1,128,256]{2,1,0:T(8,128)(2,1)S(1)} collective-permute-done((bf16[1,128,256]{2,1,0:T(8,128)(2,1)S(1)}, bf16[1,128,256]{2,1,0:T(8,128)(2,1)S(1)}, u32[]{:S(2)}, u32[]{:S(2)}) %collective-permute-start) | collective-permute-done | bytes 65568 | tf_op jit(solution)/shard_map/ppermute | solution.py:66
  86.8 0.0 collective-permute-start.1
  86.8 3.6 %collective-permute-start.4 = (bf16[1,128,256]{2,1,0:T(8,128)(2,1)S(1)}, bf16[1,128,256]{2,1,0:T(8,128)(2,1)S(1)}, u32[]{:S(2)}, u32[]{:S(2)}) collective-permute-start(bf16[1,128,256]{2,1,0:T(8,128)(2,1)S(1)} %bitcast.111), channel_id=1, source_target_pairs={{4,0},{8,4},{12,8},{16,12},{20,16},{24,20},{28,24},{0,28},{5,1},{9... | collective-permute-start | bytes 196616 | tf_op jit(solution)/shard_map/ppermute | solution.py:70
  90.4 1.9 %collective-permute-done.1 = bf16[1,128,256]{2,1,0:T(8,128)(2,1)S(1)} collective-permute-done((bf16[1,128,256]{2,1,0:T(8,128)(2,1)S(1)}, bf16[1,128,256]{2,1,0:T(8,128)(2,1)S(1)}, u32[]{:S(2)}, u32[]{:S(2)}) %collective-permute-start.1) | collective-permute-done | bytes 65568 | tf_op jit(solution)/shard_map/ppermute | solution.py:66
  92.3 0.0 collective-permute-start.2
  92.3 0.0 collective-permute-done.4
  92.3 3.6 %collective-permute-start.5 = (bf16[1,128,256]{2,1,0:T(8,128)(2,1)S(1)}, bf16[1,128,256]{2,1,0:T(8,128)(2,1)S(1)}, u32[]{:S(2)}, u32[]{:S(2)}) collective-permute-start(bf16[1,128,256]{2,1,0:T(8,128)(2,1)S(1)} %collective-permute-done.4), channel_id=1, source_target_pairs={{4,0},{8,4},{12,8},{16,12},{20,16},{24,20},{28,24},{0,28},{5,1},{9... | collective-permute-start | bytes 196616 | tf_op jit(solution)/shard_map/ppermute | solution.py:70
  95.9 1.9 %collective-permute-done.2 = bf16[1,128,256]{2,1,0:T(8,128)(2,1)S(1)} collective-permute-done((bf16[1,128,256]{2,1,0:T(8,128)(2,1)S(1)}, bf16[1,128,256]{2,1,0:T(8,128)(2,1)S(1)}, u32[]{:S(2)}, u32[]{:S(2)}) %collective-permute-start.2) | collective-permute-done | bytes 65568 | tf_op jit(solution)/shard_map/ppermute | solution.py:66
  97.8 0.0 collective-permute-start.3
  97.8 0.7 fusion.31
  98.5 0.0 collective-permute-done.5
  98.5 3.5 %collective-permute-start.6 = (bf16[1,128,256]{2,1,0:T(8,128)(2,1)S(1)}, bf16[1,128,256]{2,1,0:T(8,128)(2,1)S(1)}, u32[]{:S(2)}, u32[]{:S(2)}) collective-permute-start(bf16[1,128,256]{2,1,0:T(8,128)(2,1)S(1)} %collective-permute-done.5), channel_id=1, source_target_pairs={{4,0},{8,4},{12,8},{16,12},{20,16},{24,20},{28,24},{0,28},{5,1},{9... | collective-permute-start | bytes 196616 | tf_op jit(solution)/shard_map/ppermute | solution.py:70
  102.1 1.3 collective-permute-done.3
  103.4 0.6 collective-permute-done.6
  104.0 0.6 gather_fusion.1
  104.6 1.0 convolution_bitcast_fusion.1
  105.6 0.0 all-reduce.4.cloned.1.call-update
  105.6 0.8 copy-done.2
  106.4 0.3 fusion
  106.7 0.9 copy.19
  107.5 41.5 %all-reduce.4.cloned.1.call-done = f32[128,256]{0,1:T(8,128)} async-done(((f32[128,256]{0,1:T(8,128)}), f32[128,256]{0,1:T(8,128)}) %all-reduce.4.cloned.1.call-update) | async-done | bytes 131088 | tf_op jit(solution)/shard_map/psum | solution.py:83
  149.1 0.9 broadcast_multiply_fusion
  150.0 0.8 copy.20
  (19 shorter events, 0.1 us)
Async XLA Ops:
  7.2 1.0 copy-start
  7.2 38.3 %reduce-scatter.2.cloned.1.call-start = ((), (), s32[]{:S(2)}) async-start(), calls=%async_computation.2 | async-start | bytes 1179648 | tf_op jit(solution)/shard_map/reduce_scatter | solution.py:23
  10.2 0.9 copy-start.1
  10.3 138.8 %all-reduce.4.cloned.1.call-start = ((), (), s32[]{:S(2)}) async-start(), calls=%async_computation.3 | async-start | bytes 262144 | tf_op jit(solution)/shard_map/psum | solution.py:83
  11.4 0.7 copy-start.5
  60.6 0.7 copy-start.3
  61.3 0.8 copy-start.4
  81.2 5.5 %collective-permute-start = (bf16[1,128,256]{2,1,0:T(8,128)(2,1)S(1)}, bf16[1,128,256]{2,1,0:T(8,128)(2,1)S(1)}, u32[]{:S(2)}, u32[]{:S(2)}) collective-permute-start(bf16[1,128,256]{2,1,0:T(8,128)(2,1)S(1)} %bitcast.110), channel_id=1, source_target_pairs={{0,4},{4,8},{8,12},{12,16},{16,20},{20,24},{24,28},{28,0},{1,5},{5... | collective-permute-start | bytes 196616 | tf_op jit(solution)/shard_map/ppermute | solution.py:66
  86.8 5.6 %collective-permute-start.1 = (bf16[1,128,256]{2,1,0:T(8,128)(2,1)S(1)}, bf16[1,128,256]{2,1,0:T(8,128)(2,1)S(1)}, u32[]{:S(2)}, u32[]{:S(2)}) collective-permute-start(bf16[1,128,256]{2,1,0:T(8,128)(2,1)S(1)} %collective-permute-done), channel_id=1, source_target_pairs={{0,4},{4,8},{8,12},{12,16},{16,20},{20,24},{24,28},{28,0},{1,5},{5... | collective-permute-start | bytes 196616 | tf_op jit(solution)/shard_map/ppermute | solution.py:66
  86.8 5.6 %collective-permute-start.4 = (bf16[1,128,256]{2,1,0:T(8,128)(2,1)S(1)}, bf16[1,128,256]{2,1,0:T(8,128)(2,1)S(1)}, u32[]{:S(2)}, u32[]{:S(2)}) collective-permute-start(bf16[1,128,256]{2,1,0:T(8,128)(2,1)S(1)} %bitcast.111), channel_id=1, source_target_pairs={{4,0},{8,4},{12,8},{16,12},{20,16},{24,20},{28,24},{0,28},{5,1},{9... | collective-permute-start | bytes 196616 | tf_op jit(solution)/shard_map/ppermute | solution.py:70
  92.3 5.5 %collective-permute-start.2 = (bf16[1,128,256]{2,1,0:T(8,128)(2,1)S(1)}, bf16[1,128,256]{2,1,0:T(8,128)(2,1)S(1)}, u32[]{:S(2)}, u32[]{:S(2)}) collective-permute-start(bf16[1,128,256]{2,1,0:T(8,128)(2,1)S(1)} %collective-permute-done.1), channel_id=1, source_target_pairs={{0,4},{4,8},{8,12},{12,16},{16,20},{20,24},{24,28},{28,0},{1,5},{5... | collective-permute-start | bytes 196616 | tf_op jit(solution)/shard_map/ppermute | solution.py:66
  92.3 6.2 %collective-permute-start.5 = (bf16[1,128,256]{2,1,0:T(8,128)(2,1)S(1)}, bf16[1,128,256]{2,1,0:T(8,128)(2,1)S(1)}, u32[]{:S(2)}, u32[]{:S(2)}) collective-permute-start(bf16[1,128,256]{2,1,0:T(8,128)(2,1)S(1)} %collective-permute-done.4), channel_id=1, source_target_pairs={{4,0},{8,4},{12,8},{16,12},{20,16},{24,20},{28,24},{0,28},{5,1},{9... | collective-permute-start | bytes 196616 | tf_op jit(solution)/shard_map/ppermute | solution.py:70
  97.8 5.5 %collective-permute-start.3 = (bf16[1,128,256]{2,1,0:T(8,128)(2,1)S(1)}, bf16[1,128,256]{2,1,0:T(8,128)(2,1)S(1)}, u32[]{:S(2)}, u32[]{:S(2)}) collective-permute-start(bf16[1,128,256]{2,1,0:T(8,128)(2,1)S(1)} %collective-permute-done.2), channel_id=1, source_target_pairs={{0,4},{4,8},{8,12},{12,16},{16,20},{20,24},{24,28},{28,0},{1,5},{5... | collective-permute-start | bytes 196616 | tf_op jit(solution)/shard_map/ppermute | solution.py:66
  98.5 5.4 %collective-permute-start.6 = (bf16[1,128,256]{2,1,0:T(8,128)(2,1)S(1)}, bf16[1,128,256]{2,1,0:T(8,128)(2,1)S(1)}, u32[]{:S(2)}, u32[]{:S(2)}) collective-permute-start(bf16[1,128,256]{2,1,0:T(8,128)(2,1)S(1)} %collective-permute-done.5), channel_id=1, source_target_pairs={{4,0},{8,4},{12,8},{16,12},{20,16},{24,20},{28,24},{0,28},{5,1},{9... | collective-permute-start | bytes 196616 | tf_op jit(solution)/shard_map/ppermute | solution.py:70
  105.6 0.8 copy-start.2
Sparse Core Ops, SparseCore 0:
  10.4 35.0 reduce-scatter.1
  105.7 43.3 all-reduce.3
